TPU v7x, 32 devices: a whole 2x2x4 slice. The times are simulated.
32 devices in a mesh: gy: 8 (over y, x, core), gz: 4 (over z).
Axes of the slice: x: 2, y: 2, z: 4, core: 2. Of those that a mesh axis runs over, the one named last changes fastest.
Arguments:
- volume: float32 [64, 128, 1024], P('gz', None, 'gy'), may hold values from -6 to 6
- contrast: float32 [128], replicated, may hold values from 0.1 to 1
Outputs:
- filtered: float32 [64, 128, 1024], P('gz', None, 'gy')
All inputs are finite; a program needn't handle non-finite values.
Results may differ from a plain program's by a relative error of at most 0.0003.
Values sent between devices are 32-bit elements; how exact they have to be, the bound alone decides.
A program may use at most 192 MiB of HBM per device.

v0:
```python
import jax
import jax.numpy as jnp
from jax import lax
from jax.sharding import PartitionSpec as P

STEPS = 2
kernel_taps = (0.05448868, 0.24420134, 0.40261995, 0.24420134, 0.05448868)
half_scale = 600.0


def extended(block, sides, width):
    for axis, dim in sides:
        count = lax.axis_size(axis)
        forward = [(i, i + 1) for i in range(count - 1)]
        backward = [(target, source) for source, target in forward]
        low = lax.ppermute(
            lax.slice_in_dim(block, block.shape[dim] - width, None, axis=dim), axis, forward
        )
        high = lax.ppermute(lax.slice_in_dim(block, 0, width, axis=dim), axis, backward)
        block = jnp.concatenate([low, block, high], axis=dim)
    return block


def slice_axis(array, start, count, axis, stride=1):
    return lax.slice_in_dim(array, start, start + stride * (count - 1) + 1, stride, axis)


def reduce_solve(lower, diagonal, upper, right, axis):
    length = right.shape[axis]
    if length == 1:
        return right / diagonal
    count_even = (length + 1) // 2
    count_odd = length // 2
    evens = [slice_axis(array, 0, count_even, axis, 2) for array in (lower, diagonal, upper, right)]
    odds = [slice_axis(array, 1, count_odd, axis, 2) for array in (lower, diagonal, upper, right)]
    before = [slice_axis(array, 0, count_odd, axis) for array in evens]
    fills = [0.0, 1.0, 0.0, 0.0]
    after = [
        slice_axis(
            jnp.concatenate([array, jnp.zeros_like(slice_axis(array, 0, 1, axis)) + extra], axis),
            1,
            count_odd,
            axis,
        )
        for array, extra in zip(evens, fills)
    ]
    factor_before = -odds[0] / before[1]
    factor_after = -odds[2] / after[1]
    new_lower = factor_before * before[0]
    new_diag = odds[1] + factor_before * before[2] + factor_after * after[0]
    new_upper = factor_after * after[2]
    new_right = odds[3] + factor_before * before[3] + factor_after * after[3]
    solved_odd = reduce_solve(new_lower, new_diag, new_upper, new_right, axis)
    zero_row = jnp.zeros_like(slice_axis(solved_odd, 0, 1, axis))
    extra_rows = [zero_row] * (count_even - count_odd)
    padded_odd = jnp.concatenate([zero_row, solved_odd] + extra_rows, axis)
    left_value = slice_axis(padded_odd, 0, count_even, axis)
    right_value = slice_axis(padded_odd, 1, count_even, axis)
    solved_even = (evens[3] - evens[0] * left_value - evens[2] * right_value) / evens[1]
    odd_full = jnp.concatenate([solved_odd] + extra_rows, axis)
    paired = jnp.stack([solved_even, odd_full], axis=axis + 1)
    shape = right.shape[:axis] + (2 * count_even,) + right.shape[axis + 1 :]
    return slice_axis(paired.reshape(shape), 0, length, axis)


def line_solve(upper, right, axis):
    length = upper.shape[axis]
    lower = jnp.concatenate(
        [jnp.zeros_like(slice_axis(upper, 0, 1, axis)), slice_axis(upper, 0, length - 1, axis)],
        axis,
    )
    diagonal = 1.0 + lower + upper
    return reduce_solve(-lower, diagonal, -upper, right, axis)


def smooth_axis(padded, axis):
    count = padded.shape[axis] - 4
    total = kernel_taps[0] * slice_axis(padded, 0, count, axis)
    for offset in range(1, 5):
        total = total + kernel_taps[offset] * slice_axis(padded, offset, count, axis)
    return total


def on_device(volume, contrast):
    depth, rows, cols = volume.shape
    count_z = lax.axis_size("gz")
    count_y = lax.axis_size("gy")
    total_z = depth * count_z
    total_y = cols * count_y
    start_z = lax.axis_index("gz") * depth
    start_y = lax.axis_index("gy") * cols
    pos_z = start_z - 2 + jnp.arange(depth + 4)
    pos_y = start_y - 2 + jnp.arange(cols + 4)
    inside = ((pos_z >= 0) & (pos_z < total_z))[:, None, None] & ((pos_y >= 0) & (pos_y < total_y))[
        None, None, :
    ]
    own_z = start_z + jnp.arange(depth) < total_z - 1
    own_y = start_y + jnp.arange(cols) < total_y - 1
    contrast_squared = (contrast * contrast)[None, :, None]
    current = volume
    for repeat in range(STEPS):
        padded = extended(current, (("gy", 2), ("gz", 0)), 4)
        blurred = smooth_axis(padded, 0)
        blurred = smooth_axis(blurred, 2)
        blurred = smooth_axis(jnp.pad(blurred, ((0, 0), (2, 2), (0, 0))), 1)
        blurred = jnp.where(inside, blurred, 0.0)
        grad_z = (blurred[2:, :, 1:-1] - blurred[:-2, :, 1:-1]) * 0.5
        grad_y = (blurred[1:-1, :, 2:] - blurred[1:-1, :, :-2]) * 0.5
        widened = jnp.pad(blurred[1:-1, :, 1:-1], ((0, 0), (1, 1), (0, 0)))
        grad_x = (widened[:, 2:] - widened[:, :-2]) * 0.5
        square = grad_x * grad_x + grad_y * grad_y + grad_z * grad_z
        diffusivity = 1.0 / (1.0 + square / contrast_squared)
        center = diffusivity[1:-1, :, 1:-1]
        face_x = jnp.concatenate(
            [(center[:, :-1] + center[:, 1:]) * half_scale, jnp.zeros_like(center[:, :1])], 1
        )
        face_y = jnp.where(
            own_y[None, None, :], (center + diffusivity[1:-1, :, 2:]) * half_scale, 0.0
        )
        face_z = jnp.where(
            own_z[:, None, None], (center + diffusivity[2:, :, 1:-1]) * half_scale, 0.0
        )
        solved_x = line_solve(face_x, current, 1)
        lined_y = line_solve(
            lax.all_to_all(face_y, "gy", split_axis=1, concat_axis=2, tiled=True),
            lax.all_to_all(current, "gy", split_axis=1, concat_axis=2, tiled=True),
            2,
        )
        solved_y = lax.all_to_all(lined_y, "gy", split_axis=2, concat_axis=1, tiled=True)
        lined_z = line_solve(
            lax.all_to_all(face_z, "gz", split_axis=1, concat_axis=0, tiled=True),
            lax.all_to_all(current, "gz", split_axis=1, concat_axis=0, tiled=True),
            0,
        )
        solved_z = lax.all_to_all(lined_z, "gz", split_axis=0, concat_axis=1, tiled=True)
        current = (solved_x + solved_y + solved_z) / 3.0
    return current


def solution(mesh):
    in_specs = (P("gz", None, "gy"), P())
    out_specs = P("gz", None, "gy")
    return jax.shard_map(
        on_device, mesh=mesh, in_specs=in_specs, out_specs=out_specs, check_vma=False
    )
```

profile of v0, /device:TPU:2, one launch (start us, length us, event | category | flops | bytes accessed | tf_op | source)
XLA Modules:
  0.0 528.9 jit_solution(7200915971150292406)
XLA Ops:
  12.6 7.8 %collective-permute-done = f32[16,128,4]{1,0,2:T(8,128)S(1)} collective-permute-done((f32[16,128,4]{1,0,2:T(8,128)S(1)}, f32[16,128,4]{1,0,2:T(8,128)S(1)}, u32[]{:S(2)}, u32[]{:S(2)}) %collective-permute-start) | collective-permute-done | bytes 32800 | tf_op jit(solution)/shard_map/ppermute | solution.py:16
  30.3 9.2 %collective-permute-done.2 = f32[4,128,136]{2,0,1:T(4,128)S(1)} collective-permute-done((f32[4,128,136]{2,0,1:T(4,128)S(1)}, f32[4,128,136]{2,0,1:T(4,128)S(1)}, u32[]{:S(2)}, u32[]{:S(2)}) %collective-permute-start.2) | collective-permute-done | bytes 278560 | tf_op jit(solution)/shard_map/ppermute | solution.py:16
  46.3 4.7 fusion.53
  72.9 6.2 %copy.1330 = f32[16,16,8,128]{1,0,3,2:T(8,128)} copy(f32[16,16,8,128]{3,0,1,2:T(8,128)} %bitcast.28) | data formatting | bytes 2097152 | tf_op jit(solution)/shard_map/all_to_all | solution.py:126
  79.1 4.6 slice.2057
  85.8 4.3 all-to-all-start.3
  90.1 5.1 copy.1331
  95.2 7.2 %slice.2599 = f32[16,16,1023]{1,0,2:T(8,128)} slice(f32[16,16,1024]{1,0,2:T(8,128)} %bitcast.296), slice={[0:16], [0:16], [0:1023]} | slice | bytes 2095104 | tf_op jit(solution)/shard_map/slice | solution.py:25
  102.4 11.4 %bitcast_negate_fusion.3 = (f32[16,16,1024]{1,0,2:T(8,128)}, f32[16,16,1024]{1,0,2:T(8,128)S(1)}, f32[16,16,1024]{1,0,2:T(8,128)}) fusion(f32[16,16,8,128]{1,0,3,2:T(8,128)} %copy.1331, f32[16,16,1023]{1,0,2:T(8,128)} %slice.2599), kind=kLoop, calls=%fused_computation.938 | loop fusion | flops 1048576 | bytes 5241856 | tf_op jit(solution)/shard_map/neg | solution.py:73
  116.3 5.3 copy-done.1
  124.2 20.4 %fusion.2 = (f32[16,16,512]{1,0,2:T(8,128)}, f32[16,16,512]{1,0,2:T(8,128)}, f32[16,16,512]{1,0,2:T(8,128)}, f32[16,16,512]{1,0,2:T(8,128)}) fusion(f32[16,16,512]{1,0,2:T(8,128)} %slice.2057, f32[16,16,1024]{1,0,2:T(8,128)} %bitcast.299, f32[16,16,1024]{1,0,2:T(8,128)S(1)} %get-tuple-element.34, f32[16,16,1024]{1,0,2:T(8,128)} %get-tuple-element.35, ...), kind=kLoop, calls=%fused_computation.18 | loop fusion | flops 1835008 | bytes 7340032 | tf_op jit(solution)/shard_map/add | solution.py:52
  144.6 5.3 fusion.5
  156.2 6.8 %fusion.60 = (f32[16,16,256]{1,0,2:T(8,128)}, f32[16,16,256]{1,0,2:T(8,128)S(1)}, f32[16,16,256]{1,0,2:T(8,128)S(1)}, f32[16,16,256]{1,0,2:T(8,128)}) fusion(f32[16,16,256]{1,0,2:T(8,128)} %slice.2068, f32[16,16,512]{1,0,2:T(8,128)S(1)} %copy-done.8, f32[16,16,512]{1,0,2:T(8,128)S(1)} %copy-done.4, f32[16,16,512]{1,0,2:T(8,128)S(1)} %copy-done.5, ...), kind=kLoop, calls=%fused_computation.120 | loop fusion | flops 917504 | bytes 3670016 | tf_op jit(solution)/shard_map/add | solution.py:52
  170.5 5.7 %fusion.82 = (f32[16,16,128]{1,0,2:T(8,128)}, f32[16,16,128]{1,0,2:T(8,128)S(1)}, f32[16,16,128]{1,0,2:T(8,128)}, f32[16,16,128]{1,0,2:T(8,128)}) fusion(f32[16,16,128]{1,0,2:T(8,128)} %slice.2080, f32[16,16,256]{1,0,2:T(8,128)} %get-tuple-element.25, f32[16,16,256]{1,0,2:T(8,128)S(1)} %get-tuple-element.26, f32[16,16,256]{1,0,2:T(8,128)S(1)} %get-tuple-element.31, ...), kind=kLoop, calls=%fused_computation.156 | loop fusion | flops 458752 | bytes 1835008 | tf_op jit(solution)/shard_map/add | solution.py:52
  186.6 5.0 all-to-all-start.4
  196.1 5.9 %fusion.10 = f32[16,16,512,1]{1,0,2,3:T(8,128)S(1)} fusion(f32[16,16,512]{1,0,2:T(8,128)S(1)} %bitcast.304, f32[16,16,1024]{1,0,2:T(8,128)} %bitcast.300, f32[16,16,1024]{1,0,2:T(8,128)} %get-tuple-element.33, f32[16,16,1024]{1,0,2:T(8,128)S(1)} %bitcast.293, f32[16,16,1024]{1,0,2:T(8,128)} %get-tuple-element.35), kind=kLoop, calls=%fused_computation.26 | loop fusion | flops 655360 | bytes 3145728 | tf_op jit(solution)/shard_map/stack | solution.py:61
  202.6 4.7 copy.1259
  207.3 8.1 %reshape.239 = f32[8,1,32768]{2,1,0:T(1,128)} reshape(f32[1024,16,16]{2,1,0:T(8,128)} %bitcast.310) | data formatting | bytes 2097152
  217.8 5.6 %all-to-all-start.2 = ((f32[8,1,32768]{2,1,0:T(1,128)}), f32[8,1,32768]{2,1,0:T(1,128)}, u32[]{:S(2)}, u32[]{:S(2)}) async-start(f32[8,1,32768]{2,1,0:T(1,128)} %reshape.239), calls=%async_computation.2 | async-start | bytes 2097152 | tf_op jit(solution)/shard_map/all_to_all | solution.py:129
  229.8 7.6 %all-to-all-done.2 = f32[8,1,32768]{2,1,0:T(1,128)} async-done(((f32[8,1,32768]{2,1,0:T(1,128)}), f32[8,1,32768]{2,1,0:T(1,128)}, u32[]{:S(2)}, u32[]{:S(2)}) %all-to-all-start.2) | async-done | bytes 1048608 | tf_op jit(solution)/shard_map/all_to_all | solution.py:129
  237.4 5.5 %all-to-all-start.5 = ((f32[64,32,128]{2,1,0:T(8,128)}), f32[64,32,128]{2,1,0:T(8,128)S(1)}, u32[]{:S(2)}, u32[]{:S(2)}) async-start(f32[64,32,128]{2,1,0:T(8,128)} %bitcast.92), calls=%async_computation.5 | async-start | bytes 2097152 | tf_op jit(solution)/shard_map/all_to_all | solution.py:135
  251.9 6.2 %reshape.240 = f32[1024,16,16]{2,1,0:T(8,128)} reshape(f32[8,32768]{1,0:T(8,128)S(1)} %reduce) | data formatting | bytes 2097152
  258.1 5.7 %copy.1261 = f32[16,8,16,128]{3,0,2,1:T(8,128)S(1)} copy(f32[16,8,16,128]{2,0,3,1:T(8,128)} %bitcast.308) | data formatting | bytes 2097152 | tf_op jit(solution)/shard_map/all_to_all | solution.py:129
  263.8 5.1 all-to-all-done.5
  286.8 4.4 all-to-all-start.6
  292.3 5.3 %collective-permute-done.6 = f32[4,128,136]{2,0,1:T(4,128)S(1)} collective-permute-done((f32[4,128,136]{2,0,1:T(4,128)}, f32[4,128,136]{2,0,1:T(4,128)S(1)}, u32[]{:S(2)}, u32[]{:S(2)}) %collective-permute-start.6) | collective-permute-done | bytes 278560 | tf_op jit(solution)/shard_map/ppermute | solution.py:16
  304.3 4.7 fusion.36
  330.6 6.2 %copy.1337 = f32[16,16,8,128]{1,0,3,2:T(8,128)} copy(f32[16,16,8,128]{3,0,1,2:T(8,128)} %bitcast.124) | data formatting | bytes 2097152 | tf_op jit(solution)/shard_map/all_to_all | solution.py:126
  336.8 4.6 slice.2371
  347.8 5.1 copy.1338
  352.9 7.2 %slice.2645 = f32[16,16,1023]{1,0,2:T(8,128)} slice(f32[16,16,1024]{1,0,2:T(8,128)} %bitcast.297), slice={[0:16], [0:16], [0:1023]} | slice | bytes 2095104 | tf_op jit(solution)/shard_map/slice | solution.py:25
  360.2 11.4 %bitcast_negate_fusion.1 = (f32[16,16,1024]{1,0,2:T(8,128)}, f32[16,16,1024]{1,0,2:T(8,128)S(1)}, f32[16,16,1024]{1,0,2:T(8,128)}) fusion(f32[16,16,8,128]{1,0,3,2:T(8,128)} %copy.1338, f32[16,16,1023]{1,0,2:T(8,128)} %slice.2645), kind=kLoop, calls=%fused_computation.936 | loop fusion | flops 1048576 | bytes 5241856 | tf_op jit(solution)/shard_map/neg | solution.py:73
  374.1 5.3 copy-done.3
  381.9 20.4 %fusion.13 = (f32[16,16,512]{1,0,2:T(8,128)}, f32[16,16,512]{1,0,2:T(8,128)}, f32[16,16,512]{1,0,2:T(8,128)}, f32[16,16,512]{1,0,2:T(8,128)}) fusion(f32[16,16,512]{1,0,2:T(8,128)} %slice.2371, f32[16,16,1024]{1,0,2:T(8,128)} %bitcast.302, f32[16,16,1024]{1,0,2:T(8,128)S(1)} %get-tuple-element.30, f32[16,16,1024]{1,0,2:T(8,128)} %get-tuple-element.36, ...), kind=kLoop, calls=%fused_computation.29 | loop fusion | flops 1835008 | bytes 7340032 | tf_op jit(solution)/shard_map/add | solution.py:52
  402.4 5.3 fusion.16
  413.9 7.0 %fusion.71 = (f32[16,16,256]{1,0,2:T(8,128)}, f32[16,16,256]{1,0,2:T(8,128)S(1)}, f32[16,16,256]{1,0,2:T(8,128)S(1)}, f32[16,16,256]{1,0,2:T(8,128)}) fusion(f32[16,16,256]{1,0,2:T(8,128)} %slice.2382, f32[16,16,512]{1,0,2:T(8,128)S(1)} %copy-done.9, f32[16,16,512]{1,0,2:T(8,128)S(1)} %copy-done.6, f32[16,16,512]{1,0,2:T(8,128)S(1)} %copy-done.7, ...), kind=kLoop, calls=%fused_computation.131 | loop fusion | flops 917504 | bytes 3670016 | tf_op jit(solution)/shard_map/add | solution.py:52
  428.5 5.7 %fusion.93 = (f32[16,16,128]{1,0,2:T(8,128)}, f32[16,16,128]{1,0,2:T(8,128)S(1)}, f32[16,16,128]{1,0,2:T(8,128)}, f32[16,16,128]{1,0,2:T(8,128)}) fusion(f32[16,16,128]{1,0,2:T(8,128)} %slice.2394, f32[16,16,256]{1,0,2:T(8,128)} %get-tuple-element.23, f32[16,16,256]{1,0,2:T(8,128)S(1)} %get-tuple-element.24, f32[16,16,256]{1,0,2:T(8,128)S(1)} %get-tuple-element.27, ...), kind=kLoop, calls=%fused_computation.167 | loop fusion | flops 458752 | bytes 1835008 | tf_op jit(solution)/shard_map/add | solution.py:52
  444.6 5.0 all-to-all-start.10
  454.1 5.9 %fusion.21 = f32[16,16,512,1]{1,0,2,3:T(8,128)S(1)} fusion(f32[16,16,512]{1,0,2:T(8,128)S(1)} %bitcast.306, f32[16,16,1024]{1,0,2:T(8,128)} %bitcast.303, f32[16,16,1024]{1,0,2:T(8,128)} %get-tuple-element.29, f32[16,16,1024]{1,0,2:T(8,128)S(1)} %bitcast.295, f32[16,16,1024]{1,0,2:T(8,128)} %get-tuple-element.36), kind=kLoop, calls=%fused_computation.37 | loop fusion | flops 655360 | bytes 3145728 | tf_op jit(solution)/shard_map/stack | solution.py:61
  460.5 4.7 copy.1314
  465.2 8.1 %reshape.241 = f32[8,1,32768]{2,1,0:T(1,128)} reshape(f32[1024,16,16]{2,1,0:T(8,128)} %bitcast.311) | data formatting | bytes 2097152
  475.7 5.9 %all-to-all-start.8 = ((f32[8,1,32768]{2,1,0:T(1,128)}), f32[8,1,32768]{2,1,0:T(1,128)}, u32[]{:S(2)}, u32[]{:S(2)}) async-start(f32[8,1,32768]{2,1,0:T(1,128)} %reshape.241), calls=%async_computation.8 | async-start | bytes 2097152 | tf_op jit(solution)/shard_map/all_to_all | solution.py:129
  488.0 7.6 %all-to-all-done.8 = f32[8,1,32768]{2,1,0:T(1,128)} async-done(((f32[8,1,32768]{2,1,0:T(1,128)}), f32[8,1,32768]{2,1,0:T(1,128)}, u32[]{:S(2)}, u32[]{:S(2)}) %all-to-all-start.8) | async-done | bytes 1048608 | tf_op jit(solution)/shard_map/all_to_all | solution.py:129
  495.6 5.1 all-to-all-start.11
  504.9 4.3 reduce.1
  509.2 6.2 %reshape.242 = f32[1024,16,16]{2,1,0:T(8,128)} reshape(f32[8,32768]{1,0:T(8,128)S(1)} %reduce.1) | data formatting | bytes 2097152
  515.3 5.7 %copy.1316 = f32[16,8,16,128]{3,0,2,1:T(8,128)S(1)} copy(f32[16,8,16,128]{2,0,3,1:T(8,128)} %bitcast.309) | data formatting | bytes 2097152 | tf_op jit(solution)/shard_map/all_to_all | solution.py:129
  521.1 5.6 %all-to-all-done.11 = f32[64,32,128]{2,1,0:T(8,128)S(1)} async-done(((f32[64,32,128]{2,1,0:T(8,128)}), f32[64,32,128]{2,1,0:T(8,128)S(1)}, u32[]{:S(2)}, u32[]{:S(2)}) %all-to-all-start.11) | async-done | bytes 1048608 | tf_op jit(solution)/shard_map/all_to_all | solution.py:135
  (549 shorter events, 205.8 us)
Async XLA Ops:
  0.0 7.2 %copy-start.18 = (f32[16,128,128]{2,1,0:T(8,128)S(1)}, f32[16,128,128]{2,1,0:T(8,128)}, u32[]{:S(2)}) copy-start(f32[16,128,128]{2,1,0:T(8,128)} %param.2) | copy-start | bytes 3145732
  2.9 65.2 %all-to-all-start = ((f32[16,128,128]{2,0,1:T(8,128)}), f32[16,128,128]{2,0,1:T(8,128)}, u32[]{:S(2)}, u32[]{:S(2)}) async-start(f32[16,128,128]{2,0,1:T(8,128)} %copy.1217), calls=%async_computation | async-start | bytes 2097152 | tf_op jit(solution)/shard_map/all_to_all | solution.py:126
  7.8 13.1 %collective-permute-start.1 = (f32[16,128,4]{1,0,2:T(8,128)S(1)}, f32[16,128,4]{1,0,2:T(8,128)S(1)}, u32[]{:S(2)}, u32[]{:S(2)}) collective-permute-start(f32[16,128,4]{1,0,2:T(8,128)S(1)} %copy.1344), channel_id=1, source_target_pairs={{4,0},{8,4},{12,8},{16,12},{20,16},{24,20},{28,24},{5,1},{9,5},{13... | collective-permute-start | bytes 98312 | tf_op jit(solution)/shard_map/ppermute | solution.py:19
  10.2 10.2 %collective-permute-start = (f32[16,128,4]{1,0,2:T(8,128)S(1)}, f32[16,128,4]{1,0,2:T(8,128)S(1)}, u32[]{:S(2)}, u32[]{:S(2)}) collective-permute-start(f32[16,128,4]{1,0,2:T(8,128)S(1)} %copy.1343), channel_id=1, source_target_pairs={{0,4},{4,8},{8,12},{12,16},{16,20},{20,24},{24,28},{1,5},{5,9},{9,... | collective-permute-start | bytes 98312 | tf_op jit(solution)/shard_map/ppermute | solution.py:16
  12.5 53.3 %copy-start.69 = (pred[16]{0:T(512)(128)(4,1)}, pred[16]{0:T(512)(128)(4,1)S(1)}, u32[]{:S(2)}) copy-start(pred[16]{0:T(512)(128)(4,1)S(1)} %add_compare_fusion) | copy-start | bytes 52
  12.6 53.3 %copy-start.71 = (pred[128]{0:T(512)(128)(4,1)}, pred[128]{0:T(512)(128)(4,1)S(1)}, u32[]{:S(2)}) copy-start(pred[128]{0:T(512)(128)(4,1)S(1)} %add_compare_fusion.1) | copy-start | bytes 388
  20.9 9.3 %copy-start.75 = (f32[128]{0:T(128)S(1)}, f32[128]{0:T(128)}, u32[]{:S(2)}) copy-start(f32[128]{0:T(128)} %param.3) | copy-start | bytes 1540
  23.6 16.0 %collective-permute-start.2 = (f32[4,128,136]{2,0,1:T(4,128)S(1)}, f32[4,128,136]{2,0,1:T(4,128)S(1)}, u32[]{:S(2)}, u32[]{:S(2)}) collective-permute-start(f32[4,128,136]{2,0,1:T(4,128)S(1)} %get-tuple-element.63), channel_id=1, source_target_pairs={{0,1},{1,2},{2,3},{4,5},{5,6},{6,7},{8,9},{9,10},{10,11},{12,13},{... | collective-permute-start | bytes 835592 | tf_op jit(solution)/shard_map/ppermute | solution.py:16
  27.5 16.2 %collective-permute-start.3 = (f32[4,128,136]{2,0,1:T(4,128)S(1)}, f32[4,128,136]{2,0,1:T(4,128)S(1)}, u32[]{:S(2)}, u32[]{:S(2)}) collective-permute-start(f32[4,128,136]{2,0,1:T(4,128)S(1)} %get-tuple-element.64), channel_id=1, source_target_pairs={{1,0},{2,1},{3,2},{5,4},{6,5},{7,6},{9,8},{10,9},{11,10},{13,12},{... | collective-permute-start | bytes 835592 | tf_op jit(solution)/shard_map/ppermute | solution.py:19
  30.2 27.3 %copy-start.73 = (f32[128]{0:T(128)}, f32[128]{0:T(128)S(1)}, u32[]{:S(2)}) copy-start(f32[128]{0:T(128)S(1)} %mul.1232) | copy-start | bytes 1540
  30.3 24.2 %copy-start.67 = (pred[20,132]{1,0:T(8,128)(4,1)}, pred[20,132]{1,0:T(8,128)(4,1)S(1)}, u32[]{:S(2)}) copy-start(pred[20,132]{1,0:T(8,128)(4,1)S(1)} %broadcast_and_fusion) | copy-start | bytes 7924
  68.1 17.7 %all-to-all-start.1 = ((f32[16,128,128]{2,0,1:T(8,128)}), f32[16,128,128]{2,0,1:T(8,128)S(1)}, u32[]{:S(2)}, u32[]{:S(2)}) async-start(f32[16,128,128]{2,0,1:T(8,128)} %get-tuple-element.61), calls=%async_computation.1 | async-start | bytes 2097152 | tf_op jit(solution)/shard_map/all_to_all | solution.py:125
  85.8 100.8 %all-to-all-start.3 = ((f32[16,128,128]{2,0,1:T(8,128)}), f32[16,128,128]{2,0,1:T(8,128)}, u32[]{:S(2)}, u32[]{:S(2)}) async-start(f32[16,128,128]{2,0,1:T(8,128)} %copy.1217), calls=%async_computation.3 | async-start | bytes 2097152 | tf_op jit(solution)/shard_map/all_to_all | solution.py:132
  113.8 10.4 %copy-start = (f32[16,16,1024]{1,0,2:T(8,128)}, f32[16,16,1024]{1,0,2:T(8,128)S(1)}, u32[]{:S(2)}) copy-start(f32[16,16,1024]{1,0,2:T(8,128)S(1)} %get-tuple-element.34) | copy-start | bytes 3145732
  113.8 7.8 %copy-start.1 = (f32[16,16,1024]{1,0,2:T(8,128)S(1)}, f32[16,16,1024]{1,0,2:T(8,128)}, u32[]{:S(2)}) copy-start(f32[16,16,1024]{1,0,2:T(8,128)} %get-tuple-element.35) | copy-start | bytes 3145732
  144.6 5.9 %copy-start.4 = (f32[16,16,512]{1,0,2:T(8,128)S(1)}, f32[16,16,512]{1,0,2:T(8,128)}, u32[]{:S(2)}) copy-start(f32[16,16,512]{1,0,2:T(8,128)} %get-tuple-element.20) | copy-start | bytes 1572868
  149.9 3.1 copy-start.8
  163.0 5.3 %copy-start.12 = (f32[16,16,256]{1,0,2:T(8,128)S(1)}, f32[16,16,256]{1,0,2:T(8,128)}, u32[]{:S(2)}) copy-start(f32[16,16,256]{1,0,2:T(8,128)} %get-tuple-element.25) | copy-start | bytes 786436
  186.6 31.2 %all-to-all-start.4 = ((f32[16,128,128]{2,0,1:T(8,128)}), f32[16,128,128]{2,0,1:T(8,128)}, u32[]{:S(2)}, u32[]{:S(2)}) async-start(f32[16,128,128]{2,0,1:T(8,128)} %get-tuple-element.62), calls=%async_computation.4 | async-start | bytes 2097152 | tf_op jit(solution)/shard_map/all_to_all | solution.py:131
  191.7 2.8 slice-start
  217.8 19.7 %all-to-all-start.2 = ((f32[8,1,32768]{2,1,0:T(1,128)}), f32[8,1,32768]{2,1,0:T(1,128)}, u32[]{:S(2)}, u32[]{:S(2)}) async-start(f32[8,1,32768]{2,1,0:T(1,128)} %reshape.239), calls=%async_computation.2 | async-start | bytes 2097152 | tf_op jit(solution)/shard_map/all_to_all | solution.py:129
  228.6 14.4 %copy-start.65 = (f32[16,4,1,128]{3,0,1,2:T(8,128)S(1)}, f32[16,4,1,128]{3,0,1,2:T(8,128)}, u32[]{:S(2)}) copy-start(f32[16,4,1,128]{3,0,1,2:T(8,128)} %fusion.388) | copy-start | bytes 98308
  228.7 15.5 %copy-start.49 = (f32[16,32,128]{2,0,1:T(8,128)S(1)}, f32[16,32,128]{2,0,1:T(8,128)}, u32[]{:S(2)}) copy-start(f32[16,32,128]{2,0,1:T(8,128)} %copy-done.48) | copy-start | bytes 786436
  228.7 16.6 %copy-start.36 = (f32[16,64,128]{2,0,1:T(8,128)S(1)}, f32[16,64,128]{2,0,1:T(8,128)}, u32[]{:S(2)}) copy-start(f32[16,64,128]{2,0,1:T(8,128)} %copy-done.35) | copy-start | bytes 1572868
  228.7 16.6 %copy-start.40 = (f32[16,64,128]{2,0,1:T(8,128)S(1)}, f32[16,64,128]{2,0,1:T(8,128)}, u32[]{:S(2)}) copy-start(f32[16,64,128]{2,0,1:T(8,128)} %copy-done.39) | copy-start | bytes 1572868
  229.8 15.6 %copy-start.44 = (f32[16,64,128]{2,0,1:T(8,128)S(1)}, f32[16,64,128]{2,0,1:T(8,128)}, u32[]{:S(2)}) copy-start(f32[16,64,128]{2,0,1:T(8,128)} %copy-done.43) | copy-start | bytes 1572868
  237.4 31.4 %all-to-all-start.5 = ((f32[64,32,128]{2,1,0:T(8,128)}), f32[64,32,128]{2,1,0:T(8,128)S(1)}, u32[]{:S(2)}, u32[]{:S(2)}) async-start(f32[64,32,128]{2,1,0:T(8,128)} %bitcast.92), calls=%async_computation.5 | async-start | bytes 2097152 | tf_op jit(solution)/shard_map/all_to_all | solution.py:135
  273.0 6.0 %collective-permute-start.4 = (f32[16,128,4]{1,0,2:T(8,128)S(1)}, f32[16,128,4]{1,0,2:T(8,128)S(1)}, u32[]{:S(2)}, u32[]{:S(2)}) collective-permute-start(f32[16,128,4]{1,0,2:T(8,128)S(1)} %copy.1276), channel_id=1, source_target_pairs={{0,4},{4,8},{8,12},{12,16},{16,20},{20,24},{24,28},{1,5},{5,9},{9,... | collective-permute-start | bytes 98312 | tf_op jit(solution)/shard_map/ppermute | solution.py:16
  275.4 5.2 collective-permute-start.5
  284.2 13.4 %collective-permute-start.6 = (f32[4,128,136]{2,0,1:T(4,128)}, f32[4,128,136]{2,0,1:T(4,128)S(1)}, u32[]{:S(2)}, u32[]{:S(2)}) collective-permute-start(f32[4,128,136]{2,0,1:T(4,128)} %get-tuple-element.59), channel_id=1, source_target_pairs={{0,1},{1,2},{2,3},{4,5},{5,6},{6,7},{8,9},{9,10},{10,11},{12,13},{... | collective-permute-start | bytes 835592 | tf_op jit(solution)/shard_map/ppermute | solution.py:16
  285.5 16.1 %collective-permute-start.7 = (f32[4,128,136]{2,0,1:T(4,128)}, f32[4,128,136]{2,0,1:T(4,128)S(1)}, u32[]{:S(2)}, u32[]{:S(2)}) collective-permute-start(f32[4,128,136]{2,0,1:T(4,128)} %get-tuple-element.60), channel_id=1, source_target_pairs={{1,0},{2,1},{3,2},{5,4},{6,5},{7,6},{9,8},{10,9},{11,10},{13,12},{... | collective-permute-start | bytes 835592 | tf_op jit(solution)/shard_map/ppermute | solution.py:19
  286.8 39.4 %all-to-all-start.6 = ((f32[16,128,128]{2,0,1:T(8,128)}), f32[16,128,128]{2,0,1:T(8,128)}, u32[]{:S(2)}, u32[]{:S(2)}) async-start(f32[16,128,128]{2,0,1:T(8,128)} %fusion.111), calls=%async_computation.6 | async-start | bytes 2097152 | tf_op jit(solution)/shard_map/all_to_all | solution.py:126
  309.0 3.4 copy-start.68
  326.2 17.4 %all-to-all-start.7 = ((f32[16,128,128]{2,0,1:T(8,128)}), f32[16,128,128]{2,0,1:T(8,128)S(1)}, u32[]{:S(2)}, u32[]{:S(2)}) async-start(f32[16,128,128]{2,0,1:T(8,128)} %get-tuple-element.57), calls=%async_computation.7 | async-start | bytes 2097152 | tf_op jit(solution)/shard_map/all_to_all | solution.py:125
  343.6 101.0 %all-to-all-start.9 = ((f32[16,128,128]{2,0,1:T(8,128)}), f32[16,128,128]{2,0,1:T(8,128)}, u32[]{:S(2)}, u32[]{:S(2)}) async-start(f32[16,128,128]{2,0,1:T(8,128)} %fusion.111), calls=%async_computation.9 | async-start | bytes 2097152 | tf_op jit(solution)/shard_map/all_to_all | solution.py:132
  371.5 10.4 %copy-start.2 = (f32[16,16,1024]{1,0,2:T(8,128)}, f32[16,16,1024]{1,0,2:T(8,128)S(1)}, u32[]{:S(2)}) copy-start(f32[16,16,1024]{1,0,2:T(8,128)S(1)} %get-tuple-element.30) | copy-start | bytes 3145732
  371.5 7.8 %copy-start.3 = (f32[16,16,1024]{1,0,2:T(8,128)S(1)}, f32[16,16,1024]{1,0,2:T(8,128)}, u32[]{:S(2)}) copy-start(f32[16,16,1024]{1,0,2:T(8,128)} %get-tuple-element.36) | copy-start | bytes 3145732
  402.3 5.9 %copy-start.6 = (f32[16,16,512]{1,0,2:T(8,128)S(1)}, f32[16,16,512]{1,0,2:T(8,128)}, u32[]{:S(2)}) copy-start(f32[16,16,512]{1,0,2:T(8,128)} %get-tuple-element.18) | copy-start | bytes 1572868
  407.6 3.1 copy-start.9
  421.0 5.3 %copy-start.14 = (f32[16,16,256]{1,0,2:T(8,128)S(1)}, f32[16,16,256]{1,0,2:T(8,128)}, u32[]{:S(2)}) copy-start(f32[16,16,256]{1,0,2:T(8,128)} %get-tuple-element.23) | copy-start | bytes 786436
  444.6 31.2 %all-to-all-start.10 = ((f32[16,128,128]{2,0,1:T(8,128)}), f32[16,128,128]{2,0,1:T(8,128)}, u32[]{:S(2)}, u32[]{:S(2)}) async-start(f32[16,128,128]{2,0,1:T(8,128)} %get-tuple-element.58), calls=%async_computation.10 | async-start | bytes 2097152 | tf_op jit(solution)/shard_map/all_to_all | solution.py:131
  475.7 19.8 %all-to-all-start.8 = ((f32[8,1,32768]{2,1,0:T(1,128)}), f32[8,1,32768]{2,1,0:T(1,128)}, u32[]{:S(2)}, u32[]{:S(2)}) async-start(f32[8,1,32768]{2,1,0:T(1,128)} %reshape.241), calls=%async_computation.8 | async-start | bytes 2097152 | tf_op jit(solution)/shard_map/all_to_all | solution.py:129
  486.8 13.9 %copy-start.66 = (f32[16,4,1,128]{3,0,1,2:T(8,128)S(1)}, f32[16,4,1,128]{3,0,1,2:T(8,128)}, u32[]{:S(2)}) copy-start(f32[16,4,1,128]{3,0,1,2:T(8,128)} %fusion.410) | copy-start | bytes 98308
  486.9 15.0 %copy-start.46 = (f32[16,32,128]{2,0,1:T(8,128)S(1)}, f32[16,32,128]{2,0,1:T(8,128)}, u32[]{:S(2)}) copy-start(f32[16,32,128]{2,0,1:T(8,128)} %copy-done.45) | copy-start | bytes 786436
  486.9 16.1 %copy-start.34 = (f32[16,64,128]{2,0,1:T(8,128)S(1)}, f32[16,64,128]{2,0,1:T(8,128)}, u32[]{:S(2)}) copy-start(f32[16,64,128]{2,0,1:T(8,128)} %copy-done.33) | copy-start | bytes 1572868
  486.9 16.1 %copy-start.38 = (f32[16,64,128]{2,0,1:T(8,128)S(1)}, f32[16,64,128]{2,0,1:T(8,128)}, u32[]{:S(2)}) copy-start(f32[16,64,128]{2,0,1:T(8,128)} %copy-done.37) | copy-start | bytes 1572868
  488.0 15.1 %copy-start.42 = (f32[16,64,128]{2,0,1:T(8,128)S(1)}, f32[16,64,128]{2,0,1:T(8,128)}, u32[]{:S(2)}) copy-start(f32[16,64,128]{2,0,1:T(8,128)} %copy-done.41) | copy-start | bytes 1572868
  495.6 31.0 %all-to-all-start.11 = ((f32[64,32,128]{2,1,0:T(8,128)}), f32[64,32,128]{2,1,0:T(8,128)S(1)}, u32[]{:S(2)}, u32[]{:S(2)}) async-start(f32[64,32,128]{2,1,0:T(8,128)} %bitcast.188), calls=%async_computation.11 | async-start | bytes 2097152 | tf_op jit(solution)/shard_map/all_to_all | solution.py:135
  (52 other events, 80.6 us)
where the time goes:
time: 535 us; the launch traced here: 529 us
  other arithmetic  213 us (40%)
  local copies, waits for them, and re-layouts  176 us (33%)
  starting transfers between devices  75.1 us (14%)
  waiting for transfers between devices  61.7 us (12%)
    add x40, other arithmetic, reduce_solve(): new_right = odds[3] + factor_before * before[3] + factor_after * after[3]  74.7 us
    unnamed x167, local copies, waits for them, and re-layouts  56.3 us
    slice x124, local copies, waits for them, and re-layouts, slice_axis(): lax.slice_in_dim(array, start, start + stride * (count - 1) + 1, stride,...  55.3 us
    another operation x86, other arithmetic, reduce_solve(): paired = jnp.stack([solved_even, odd_full], axis=axis + 1)  35.7 us
    mul x40, other arithmetic, reduce_solve(): new_upper = factor_after * after[2]  25 us
    neg x6, other arithmetic, line_solve(): return reduce_solve(-lower, diagonal, -upper, right, axis)  24 us
    ppermute x4, waiting for transfers between devices, extended(): lax.ppermute(lax.slice_in_dim(block, block.shape[dim] - width, None, axis...  22.3 us
    add x4, other arithmetic, smooth_axis(): total + kernel_taps[offset] * slice_axis(padded, offset, count, axis)  16.2 us
  transfers between devices with their start and end apart: 20, of which 12 were waited for; matrix products, arithmetic and copies ran while one was open for 67% of the time, Pallas kernels for 0%

commit v1 on v0

--- a/solution.py
+++ b/solution.py
@@ -6,6 +6,21 @@
 STEPS = 2
 kernel_taps = (0.05448868, 0.24420134, 0.40261995, 0.24420134, 0.05448868)
 half_scale = 600.0
+
+
+def expand_knots(work_x, where_dim, here_x):
+    spare, newest = (work_x.shape[:where_dim], work_x.shape[where_dim + 1 :])
+    return jnp.moveaxis(work_x.reshape(*spare, here_x, -1, *newest), where_dim, 0)
+
+
+def watch_the_floor(frame, dimension_no):
+    frame = jnp.moveaxis(frame, 0, dimension_no)
+    w_next = frame.shape
+    return frame.reshape(
+        *w_next[:dimension_no],
+        w_next[dimension_no] * w_next[dimension_no + 1],
+        *w_next[dimension_no + 2 :]
+    )
 
 
 def extended(block, sides, width):
@@ -127,8 +142,27 @@
             2,
         )
         solved_y = lax.all_to_all(lined_y, "gy", split_axis=2, concat_axis=1, tiled=True)
+
+        def _map_targets(my_data, z_in, body, across):
+            all_values, shaped = (lax.axis_size(across), lax.axis_index(across))
+            e_now = expand_knots(my_data, body, all_values)
+            items = [e_now[shaped]]
+            no = 1
+            while no < all_values:
+                met_up = e_now[shaped ^ no]
+                items.append(
+                    lax.ppermute(
+                        met_up,
+                        axis_name=across,
+                        perm=[(dev_j, dev_j ^ no) for dev_j in range(all_values)],
+                    )
+                )
+                no = no + 1
+            e_now = jnp.stack(items)[shaped ^ jnp.arange(all_values)]
+            return watch_the_floor(e_now, z_in)
+
         lined_z = line_solve(
-            lax.all_to_all(face_z, "gz", split_axis=1, concat_axis=0, tiled=True),
+            _map_targets(face_z, 0, 1, "gz"),
             lax.all_to_all(current, "gz", split_axis=1, concat_axis=0, tiled=True),
             0,
         )

time: 535 us -> 579 us (1.082)
  other arithmetic: 213 us -> 235 us
  waiting for transfers between devices: 61.7 us -> 75.1 us
  local copies, waits for them, and re-layouts: 176 us -> 187 us
    ppermute x0 -> x6, waiting for transfers between devices: none -> 24.4 us  [_map_targets(): lax.ppermute(met_up, axis_name=across, perm=[(dev_j, dev_j ^ no) for dev_...]
    all_to_all x2 -> x0, starting transfers between devices: 10.1 us -> none  [on_device(): lax.all_to_all(face_z, 'gz', split_axis=1, concat_axis=0, tiled=True)]
    ppermute x0 -> x6, starting transfers between devices: none -> 8.77 us  [_map_targets(): lax.ppermute(met_up, axis_name=across, perm=[(dev_j, dev_j ^ no) for dev_...]
    unnamed x167 -> x203, local copies, waits for them, and re-layouts: 56.3 us -> 63.2 us
  transfers between devices with their start and end apart: 20 -> 24, of which waited for: 12 -> 14; matrix products, arithmetic and copies ran while one was open for 67% -> 67% of each run, Pallas kernels for 0% -> 0%
where the time goes in v1:
time: 579 us; the launch traced here: 573 us
  other arithmetic  235 us (41%)
  local copies, waits for them, and re-layouts  187 us (32%)
  waiting for transfers between devices  75.1 us (13%)
  starting transfers between devices  72.5 us (13%)
    add x40, other arithmetic, reduce_solve(): new_right = odds[3] + factor_before * before[3] + factor_after * after[3]  79.1 us
    unnamed x203, local copies, waits for them, and re-layouts  63.2 us
    slice x124, local copies, waits for them, and re-layouts, slice_axis(): lax.slice_in_dim(array, start, start + stride * (count - 1) + 1, stride,...  57.3 us
    another operation x86, other arithmetic, reduce_solve(): paired = jnp.stack([solved_even, odd_full], axis=axis + 1)  38.7 us
    mul x40, other arithmetic, reduce_solve(): new_upper = factor_after * after[2]  30.3 us
    neg x6, other arithmetic, line_solve(): return reduce_solve(-lower, diagonal, -upper, right, axis)  25.9 us
    ppermute x6, waiting for transfers between devices, _map_targets(): lax.ppermute(met_up, axis_name=across, perm=[(dev_j, dev_j ^ no) for dev_...  24.4 us
    ppermute x4, waiting for transfers between devices, extended(): lax.ppermute(lax.slice_in_dim(block, block.shape[dim] - width, None, axis...  17.2 us
  transfers between devices with their start and end apart: 24, of which 14 were waited for; matrix products, arithmetic and copies ran while one was open for 67% of the time, Pallas kernels for 0%

profile of v1, /device:TPU:2, one launch (start us, length us, event | category | flops | bytes accessed | tf_op | source)
XLA Modules:
  0.0 573.1 jit_solution(17970712836092465713)
XLA Ops:
  14.8 5.6 collective-permute-done
  24.5 4.3 collective-permute-start.2
  32.3 8.1 %collective-permute-done.2 = f32[4,128,136]{2,0,1:T(4,128)} collective-permute-done((f32[4,128,136]{2,0,1:T(4,128)}, f32[4,128,136]{2,0,1:T(4,128)}, u32[]{:S(2)}, u32[]{:S(2)}) %collective-permute-start.2) | collective-permute-done | bytes 278560 | tf_op jit(solution)/shard_map/ppermute | solution.py:31
  40.4 4.9 collective-permute-done.3
  48.2 4.6 fusion.53
  83.0 9.8 %collective-permute-done.5 = f32[16,32,128]{2,1,0:T(8,128)} collective-permute-done((f32[16,32,128]{2,1,0:T(8,128)}, f32[16,32,128]{2,1,0:T(8,128)}, u32[]{:S(2)}, u32[]{:S(2)}) %collective-permute-start.5) | collective-permute-done | bytes 262176 | tf_op jit(solution)/shard_map/ppermute | solution.py:154
  100.9 5.0 copy.1376
  105.9 4.5 slice.2057
  114.7 5.0 copy.1377
  119.8 7.2 %slice.2603 = f32[16,16,1023]{1,0,2:T(8,128)} slice(f32[16,16,1024]{1,0,2:T(8,128)} %bitcast.324), slice={[0:16], [0:16], [0:1023]} | slice | bytes 2095104 | tf_op jit(solution)/shard_map/slice | solution.py:40
  127.0 11.4 %bitcast_negate_fusion.3 = (f32[16,16,1024]{1,0,2:T(8,128)}, f32[16,16,1024]{1,0,2:T(8,128)S(1)}, f32[16,16,1024]{1,0,2:T(8,128)}) fusion(f32[16,16,8,128]{1,0,3,2:T(8,128)} %copy.1377, f32[16,16,1023]{1,0,2:T(8,128)} %slice.2603), kind=kLoop, calls=%fused_computation.961 | loop fusion | flops 1048576 | bytes 5241856 | tf_op jit(solution)/shard_map/neg | solution.py:88
  145.7 20.0 %fusion.2 = (f32[16,16,512]{1,0,2:T(8,128)}, f32[16,16,512]{1,0,2:T(8,128)}, f32[16,16,512]{1,0,2:T(8,128)}, f32[16,16,512]{1,0,2:T(8,128)}) fusion(f32[16,16,512]{1,0,2:T(8,128)} %slice.2057, f32[16,16,1024]{1,0,2:T(8,128)} %bitcast.327, f32[16,16,1024]{1,0,2:T(8,128)S(1)} %get-tuple-element.34, f32[16,16,1024]{1,0,2:T(8,128)} %get-tuple-element.35, ...), kind=kLoop, calls=%fused_computation.20 | loop fusion | flops 1835008 | bytes 7340032 | tf_op jit(solution)/shard_map/add | solution.py:67
  165.7 7.4 %fusion.5 = f32[16,16,512]{1,0,2:T(8,128)} fusion(f32[16,16,512]{1,0,2:T(8,128)} %get-tuple-element.32, f32[16,16,512]{1,0,2:T(8,128)} %slice.2064, f32[16,16,1024]{1,0,2:T(8,128)} %get-tuple-element.33), kind=kLoop, calls=%fused_computation.23 | loop fusion | flops 393216 | bytes 2097152 | tf_op jit(solution)/shard_map/mul | solution.py:66
  179.2 9.3 %fusion.60 = (f32[16,16,256]{1,0,2:T(8,128)}, f32[16,16,256]{1,0,2:T(8,128)S(1)}, f32[16,16,256]{1,0,2:T(8,128)S(1)}, f32[16,16,256]{1,0,2:T(8,128)}) fusion(f32[16,16,256]{1,0,2:T(8,128)} %slice.2068, f32[16,16,512]{1,0,2:T(8,128)} %get-tuple-element.19, f32[16,16,512]{1,0,2:T(8,128)S(1)} %copy-done.2, f32[16,16,512]{1,0,2:T(8,128)S(1)} %copy-done.3, ...), kind=kLoop, calls=%fused_computation.122 | loop fusion | flops 917504 | bytes 3670016 | tf_op jit(solution)/shard_map/add | solution.py:67
  188.5 4.8 fusion.63
  196.6 6.2 %fusion.82 = (f32[16,16,128]{1,0,2:T(8,128)}, f32[16,16,128]{1,0,2:T(8,128)}, f32[16,16,128]{1,0,2:T(8,128)}, f32[16,16,128]{1,0,2:T(8,128)}) fusion(f32[16,16,128]{1,0,2:T(8,128)} %slice.2080, f32[16,16,256]{1,0,2:T(8,128)} %get-tuple-element.25, f32[16,16,256]{1,0,2:T(8,128)S(1)} %get-tuple-element.26, f32[16,16,256]{1,0,2:T(8,128)S(1)} %get-tuple-element.31, ...), kind=kLoop, calls=%fused_computation.158 | loop fusion | flops 458752 | bytes 1835008 | tf_op jit(solution)/shard_map/add | solution.py:67
  219.1 6.2 %fusion.10 = f32[16,16,512,1]{1,0,2,3:T(8,128)} fusion(f32[16,16,512]{1,0,2:T(8,128)S(1)} %bitcast.332, f32[16,16,1024]{1,0,2:T(8,128)} %bitcast.328, f32[16,16,1024]{1,0,2:T(8,128)} %get-tuple-element.33, f32[16,16,1024]{1,0,2:T(8,128)S(1)} %get-tuple-element.34, f32[16,16,1024]{1,0,2:T(8,128)S(1)} %bitcast.321), kind=kLoop, calls=%fused_computation.28 | loop fusion | flops 655360 | bytes 3145728 | tf_op jit(solution)/shard_map/stack | solution.py:76
  228.0 4.7 copy.1299
  232.7 8.1 %reshape.301 = f32[8,1,32768]{2,1,0:T(1,128)} reshape(f32[1024,16,16]{2,1,0:T(8,128)} %bitcast.338) | data formatting | bytes 2097152
  240.9 4.7 all-to-all-start.2
  251.0 7.6 %all-to-all-done.2 = f32[8,1,32768]{2,1,0:T(1,128)} async-done(((f32[8,1,32768]{2,1,0:T(1,128)}), f32[8,1,32768]{2,1,0:T(1,128)}, u32[]{:S(2)}, u32[]{:S(2)}) %all-to-all-start.2) | async-done | bytes 1048608 | tf_op jit(solution)/shard_map/all_to_all | solution.py:144
  258.6 5.0 all-to-all-start.4
  270.1 4.3 reduce
  274.5 6.2 %reshape.302 = f32[1024,16,16]{2,1,0:T(8,128)} reshape(f32[8,32768]{1,0:T(8,128)S(1)} %reduce) | data formatting | bytes 2097152
  280.7 5.7 copy.1301
  309.5 4.9 all-to-all-start.5
  319.0 5.5 collective-permute-done.10
  327.5 4.5 fusion.36
  364.1 9.0 %collective-permute-done.12 = f32[16,32,128]{2,1,0:T(8,128)} collective-permute-done((f32[16,32,128]{2,1,0:T(8,128)}, f32[16,32,128]{2,1,0:T(8,128)}, u32[]{:S(2)}, u32[]{:S(2)}) %collective-permute-start.12) | collective-permute-done | bytes 262176 | tf_op jit(solution)/shard_map/ppermute | solution.py:154
  381.2 5.0 copy.1383
  386.2 4.5 slice.2371
  395.0 5.0 copy.1384
  400.0 7.2 %slice.2649 = f32[16,16,1023]{1,0,2:T(8,128)} slice(f32[16,16,1024]{1,0,2:T(8,128)} %bitcast.325), slice={[0:16], [0:16], [0:1023]} | slice | bytes 2095104 | tf_op jit(solution)/shard_map/slice | solution.py:40
  407.3 11.4 %bitcast_negate_fusion.1 = (f32[16,16,1024]{1,0,2:T(8,128)}, f32[16,16,1024]{1,0,2:T(8,128)S(1)}, f32[16,16,1024]{1,0,2:T(8,128)}) fusion(f32[16,16,8,128]{1,0,3,2:T(8,128)} %copy.1384, f32[16,16,1023]{1,0,2:T(8,128)} %slice.2649), kind=kLoop, calls=%fused_computation.959 | loop fusion | flops 1048576 | bytes 5241856 | tf_op jit(solution)/shard_map/neg | solution.py:88
  426.0 20.0 %fusion.13 = (f32[16,16,512]{1,0,2:T(8,128)}, f32[16,16,512]{1,0,2:T(8,128)}, f32[16,16,512]{1,0,2:T(8,128)}, f32[16,16,512]{1,0,2:T(8,128)}) fusion(f32[16,16,512]{1,0,2:T(8,128)} %slice.2371, f32[16,16,1024]{1,0,2:T(8,128)} %bitcast.330, f32[16,16,1024]{1,0,2:T(8,128)S(1)} %get-tuple-element.30, f32[16,16,1024]{1,0,2:T(8,128)} %get-tuple-element.36, ...), kind=kLoop, calls=%fused_computation.31 | loop fusion | flops 1835008 | bytes 7340032 | tf_op jit(solution)/shard_map/add | solution.py:67
  446.0 7.4 %fusion.16 = f32[16,16,512]{1,0,2:T(8,128)} fusion(f32[16,16,512]{1,0,2:T(8,128)} %get-tuple-element.28, f32[16,16,512]{1,0,2:T(8,128)} %slice.2378, f32[16,16,1024]{1,0,2:T(8,128)} %get-tuple-element.29), kind=kLoop, calls=%fused_computation.34 | loop fusion | flops 393216 | bytes 2097152 | tf_op jit(solution)/shard_map/mul | solution.py:66
  459.5 9.1 %fusion.71 = (f32[16,16,256]{1,0,2:T(8,128)}, f32[16,16,256]{1,0,2:T(8,128)S(1)}, f32[16,16,256]{1,0,2:T(8,128)S(1)}, f32[16,16,256]{1,0,2:T(8,128)}) fusion(f32[16,16,256]{1,0,2:T(8,128)} %slice.2382, f32[16,16,512]{1,0,2:T(8,128)} %get-tuple-element.17, f32[16,16,512]{1,0,2:T(8,128)S(1)} %copy-done.4, f32[16,16,512]{1,0,2:T(8,128)S(1)} %copy-done.5, ...), kind=kLoop, calls=%fused_computation.133 | loop fusion | flops 917504 | bytes 3670016 | tf_op jit(solution)/shard_map/add | solution.py:67
  468.6 4.8 fusion.74
  476.6 6.0 %fusion.93 = (f32[16,16,128]{1,0,2:T(8,128)}, f32[16,16,128]{1,0,2:T(8,128)}, f32[16,16,128]{1,0,2:T(8,128)}, f32[16,16,128]{1,0,2:T(8,128)}) fusion(f32[16,16,128]{1,0,2:T(8,128)} %slice.2394, f32[16,16,256]{1,0,2:T(8,128)} %get-tuple-element.23, f32[16,16,256]{1,0,2:T(8,128)S(1)} %get-tuple-element.24, f32[16,16,256]{1,0,2:T(8,128)S(1)} %get-tuple-element.27, ...), kind=kLoop, calls=%fused_computation.169 | loop fusion | flops 458752 | bytes 1835008 | tf_op jit(solution)/shard_map/add | solution.py:67
  498.9 6.2 %fusion.21 = f32[16,16,512,1]{1,0,2,3:T(8,128)} fusion(f32[16,16,512]{1,0,2:T(8,128)S(1)} %bitcast.334, f32[16,16,1024]{1,0,2:T(8,128)} %bitcast.331, f32[16,16,1024]{1,0,2:T(8,128)} %get-tuple-element.29, f32[16,16,1024]{1,0,2:T(8,128)S(1)} %get-tuple-element.30, f32[16,16,1024]{1,0,2:T(8,128)S(1)} %bitcast.323), kind=kLoop, calls=%fused_computation.39 | loop fusion | flops 655360 | bytes 3145728 | tf_op jit(solution)/shard_map/stack | solution.py:76
  507.8 4.7 copy.1357
  512.5 8.1 %reshape.303 = f32[8,1,32768]{2,1,0:T(1,128)} reshape(f32[1024,16,16]{2,1,0:T(8,128)} %bitcast.339) | data formatting | bytes 2097152
  520.7 4.7 all-to-all-start.7
  530.8 7.6 %all-to-all-done.7 = f32[8,1,32768]{2,1,0:T(1,128)} async-done(((f32[8,1,32768]{2,1,0:T(1,128)}), f32[8,1,32768]{2,1,0:T(1,128)}, u32[]{:S(2)}, u32[]{:S(2)}) %all-to-all-start.7) | async-done | bytes 1048608 | tf_op jit(solution)/shard_map/all_to_all | solution.py:144
  538.4 5.0 all-to-all-start.9
  549.4 4.3 reduce.1
  553.8 6.2 %reshape.304 = f32[1024,16,16]{2,1,0:T(8,128)} reshape(f32[8,32768]{1,0:T(8,128)S(1)} %reduce.1) | data formatting | bytes 2097152
  560.0 5.7 copy.1359
  (599 shorter events, 242.2 us)
Async XLA Ops:
  0.0 7.2 %copy-start.30 = (f32[16,128,128]{2,1,0:T(8,128)S(1)}, f32[16,128,128]{2,1,0:T(8,128)}, u32[]{:S(2)}) copy-start(f32[16,128,128]{2,1,0:T(8,128)} %param.2) | copy-start | bytes 3145732
  2.9 73.6 %all-to-all-start = ((f32[16,128,128]{2,0,1:T(8,128)}), f32[16,128,128]{2,0,1:T(8,128)S(1)}, u32[]{:S(2)}, u32[]{:S(2)}) async-start(f32[16,128,128]{2,0,1:T(8,128)} %copy.1257), calls=%async_computation | async-start | bytes 2097152 | tf_op jit(solution)/shard_map/all_to_all | solution.py:141
  10.0 10.9 %collective-permute-start.1 = (f32[16,128,4]{1,0,2:T(8,128)S(1)}, f32[16,128,4]{1,0,2:T(8,128)S(1)}, u32[]{:S(2)}, u32[]{:S(2)}) collective-permute-start(f32[16,128,4]{1,0,2:T(8,128)S(1)} %copy.1390), channel_id=1, source_target_pairs={{4,0},{8,4},{12,8},{16,12},{20,16},{24,20},{28,24},{5,1},{9,5},{13... | collective-permute-start | bytes 98312 | tf_op jit(solution)/shard_map/ppermute | solution.py:34
  12.4 8.0 %collective-permute-start = (f32[16,128,4]{1,0,2:T(8,128)S(1)}, f32[16,128,4]{1,0,2:T(8,128)S(1)}, u32[]{:S(2)}, u32[]{:S(2)}) collective-permute-start(f32[16,128,4]{1,0,2:T(8,128)S(1)} %copy.1389), channel_id=1, source_target_pairs={{0,4},{4,8},{8,12},{12,16},{16,20},{20,24},{24,28},{1,5},{5,9},{9,... | collective-permute-start | bytes 98312 | tf_op jit(solution)/shard_map/ppermute | solution.py:31
  14.7 48.5 %copy-start.83 = (pred[16]{0:T(512)(128)(4,1)}, pred[16]{0:T(512)(128)(4,1)S(1)}, u32[]{:S(2)}) copy-start(pred[16]{0:T(512)(128)(4,1)S(1)} %add_compare_fusion) | copy-start | bytes 52
  14.8 48.5 %copy-start.85 = (pred[128]{0:T(512)(128)(4,1)}, pred[128]{0:T(512)(128)(4,1)S(1)}, u32[]{:S(2)}) copy-start(pred[128]{0:T(512)(128)(4,1)S(1)} %add_compare_fusion.1) | copy-start | bytes 388
  14.8 80.2 %copy-start.82 = (s32[1024]{0:T(1024)}, s32[1024]{0:T(1024)S(1)}, u32[]{:S(2)}) copy-start(s32[1024]{0:T(1024)S(1)} %pad_clamp_fusion) | copy-start | bytes 12292
  20.9 11.3 %copy-start.89 = (f32[128]{0:T(128)S(1)}, f32[128]{0:T(128)}, u32[]{:S(2)}) copy-start(f32[128]{0:T(128)} %param.3) | copy-start | bytes 1540
  24.5 15.8 %collective-permute-start.2 = (f32[4,128,136]{2,0,1:T(4,128)}, f32[4,128,136]{2,0,1:T(4,128)}, u32[]{:S(2)}, u32[]{:S(2)}) collective-permute-start(f32[4,128,136]{2,0,1:T(4,128)} %get-tuple-element.63), channel_id=1, source_target_pairs={{0,1},{1,2},{2,3},{4,5},{5,6},{6,7},{8,9},{9,10},{10,11},{12,13},{... | collective-permute-start | bytes 835592 | tf_op jit(solution)/shard_map/ppermute | solution.py:31
  28.8 16.5 %collective-permute-start.3 = (f32[4,128,136]{2,0,1:T(4,128)}, f32[4,128,136]{2,0,1:T(4,128)}, u32[]{:S(2)}, u32[]{:S(2)}) collective-permute-start(f32[4,128,136]{2,0,1:T(4,128)} %get-tuple-element.64), channel_id=1, source_target_pairs={{1,0},{2,1},{3,2},{5,4},{6,5},{7,6},{9,8},{10,9},{11,10},{13,12},{... | collective-permute-start | bytes 835592 | tf_op jit(solution)/shard_map/ppermute | solution.py:34
  32.2 27.1 %copy-start.87 = (f32[128]{0:T(128)}, f32[128]{0:T(128)S(1)}, u32[]{:S(2)}) copy-start(f32[128]{0:T(128)S(1)} %mul.1232) | copy-start | bytes 1540
  32.3 23.9 %copy-start.80 = (pred[20,132]{1,0:T(8,128)(4,1)}, pred[20,132]{1,0:T(8,128)(4,1)S(1)}, u32[]{:S(2)}) copy-start(pred[20,132]{1,0:T(8,128)(4,1)S(1)} %broadcast_and_fusion) | copy-start | bytes 7924
  67.6 13.4 %collective-permute-start.6 = (f32[16,32,128]{2,1,0:T(8,128)}, f32[16,32,128]{2,1,0:T(8,128)}, u32[]{:S(2)}, u32[]{:S(2)}) collective-permute-start(f32[16,32,128]{2,1,0:T(8,128)} %bitcast.316), channel_id=1, source_target_pairs={{0,3},{1,2},{2,1},{3,0},{4,7},{5,6},{6,5},{7,4},{8,11},{9,10},{10,... | collective-permute-start | bytes 786440 | tf_op jit(solution)/shard_map/ppermute | solution.py:154
  68.4 14.6 %collective-permute-start.4 = (f32[16,32,128]{2,1,0:T(8,128)}, f32[16,32,128]{2,1,0:T(8,128)}, u32[]{:S(2)}, u32[]{:S(2)}) collective-permute-start(f32[16,32,128]{2,1,0:T(8,128)} %bitcast.318), channel_id=1, source_target_pairs={{0,1},{1,0},{2,3},{3,2},{4,5},{5,4},{6,7},{7,6},{8,9},{9,8},{10,11... | collective-permute-start | bytes 786440 | tf_op jit(solution)/shard_map/ppermute | solution.py:154
  70.0 22.9 %collective-permute-start.5 = (f32[16,32,128]{2,1,0:T(8,128)}, f32[16,32,128]{2,1,0:T(8,128)}, u32[]{:S(2)}, u32[]{:S(2)}) collective-permute-start(f32[16,32,128]{2,1,0:T(8,128)} %bitcast.317), channel_id=1, source_target_pairs={{0,2},{1,3},{2,0},{3,1},{4,6},{5,7},{6,4},{7,5},{8,10},{9,11},{10,... | collective-permute-start | bytes 786440 | tf_op jit(solution)/shard_map/ppermute | solution.py:154
  76.4 34.0 %all-to-all-start.1 = ((f32[16,128,128]{2,0,1:T(8,128)}), f32[16,128,128]{2,0,1:T(8,128)S(1)}, u32[]{:S(2)}, u32[]{:S(2)}) async-start(f32[16,128,128]{2,0,1:T(8,128)} %get-tuple-element.61), calls=%async_computation.1 | async-start | bytes 2097152 | tf_op jit(solution)/shard_map/all_to_all | solution.py:140
  80.3 12.5 %copy-start.79 = (f32[16,2,2,128]{3,0,2,1:T(8,128)}, f32[16,2,2,128]{3,0,2,1:T(8,128)S(1)}, u32[]{:S(2)}) copy-start(f32[16,2,2,128]{3,0,2,1:T(8,128)S(1)} %copy.1264) | copy-start | bytes 98308
  110.4 130.4 %all-to-all-start.3 = ((f32[16,128,128]{2,0,1:T(8,128)}), f32[16,128,128]{2,0,1:T(8,128)}, u32[]{:S(2)}, u32[]{:S(2)}) async-start(f32[16,128,128]{2,0,1:T(8,128)} %copy.1257), calls=%async_computation.3 | async-start | bytes 2097152 | tf_op jit(solution)/shard_map/all_to_all | solution.py:166
  165.7 7.4 %copy-start.2 = (f32[16,16,512]{1,0,2:T(8,128)S(1)}, f32[16,16,512]{1,0,2:T(8,128)}, u32[]{:S(2)}) copy-start(f32[16,16,512]{1,0,2:T(8,128)} %get-tuple-element.20) | copy-start | bytes 1572868
  240.8 6.4 %copy-start.23 = (f32[64,32,128]{2,1,0:T(8,128)S(1)}, f32[64,32,128]{2,1,0:T(8,128)}, u32[]{:S(2)}) copy-start(f32[64,32,128]{2,1,0:T(8,128)} %copy-done.22) | copy-start | bytes 3145732
  240.8 6.4 %copy-start.28 = (f32[64,32,128]{2,1,0:T(8,128)S(1)}, f32[64,32,128]{2,1,0:T(8,128)}, u32[]{:S(2)}) copy-start(f32[64,32,128]{2,1,0:T(8,128)} %get-tuple-element.105) | copy-start | bytes 3145732
  240.9 17.8 %all-to-all-start.2 = ((f32[8,1,32768]{2,1,0:T(1,128)}), f32[8,1,32768]{2,1,0:T(1,128)}, u32[]{:S(2)}, u32[]{:S(2)}) async-start(f32[8,1,32768]{2,1,0:T(1,128)} %reshape.301), calls=%async_computation.2 | async-start | bytes 2097152 | tf_op jit(solution)/shard_map/all_to_all | solution.py:144
  249.9 16.9 %copy-start.50 = (f32[16,64,128]{2,0,1:T(8,128)S(1)}, f32[16,64,128]{2,0,1:T(8,128)}, u32[]{:S(2)}) copy-start(f32[16,64,128]{2,0,1:T(8,128)} %copy-done.49) | copy-start | bytes 1572868
  249.9 16.9 %copy-start.52 = (f32[16,64,128]{2,0,1:T(8,128)S(1)}, f32[16,64,128]{2,0,1:T(8,128)}, u32[]{:S(2)}) copy-start(f32[16,64,128]{2,0,1:T(8,128)} %copy-done.51) | copy-start | bytes 1572868
  249.9 16.9 %copy-start.58 = (f32[16,64,128]{2,0,1:T(8,128)S(1)}, f32[16,64,128]{2,0,1:T(8,128)}, u32[]{:S(2)}) copy-start(f32[16,64,128]{2,0,1:T(8,128)} %copy-done.57) | copy-start | bytes 1572868
  249.9 16.9 %copy-start.62 = (f32[16,64,128]{2,0,1:T(8,128)S(1)}, f32[16,64,128]{2,0,1:T(8,128)}, u32[]{:S(2)}) copy-start(f32[16,64,128]{2,0,1:T(8,128)} %copy-done.61) | copy-start | bytes 1572868
  258.6 30.9 %all-to-all-start.4 = ((f32[64,32,128]{2,1,0:T(8,128)}), f32[64,32,128]{2,1,0:T(8,128)S(1)}, u32[]{:S(2)}, u32[]{:S(2)}) async-start(f32[64,32,128]{2,1,0:T(8,128)} %bitcast.98), calls=%async_computation.4 | async-start | bytes 2097152 | tf_op jit(solution)/shard_map/all_to_all | solution.py:169
  295.0 6.0 %collective-permute-start.7 = (f32[16,128,4]{1,0,2:T(8,128)S(1)}, f32[16,128,4]{1,0,2:T(8,128)S(1)}, u32[]{:S(2)}, u32[]{:S(2)}) collective-permute-start(f32[16,128,4]{1,0,2:T(8,128)S(1)} %copy.1319), channel_id=1, source_target_pairs={{0,4},{4,8},{8,12},{12,16},{16,20},{20,24},{24,28},{1,5},{5,9},{9,... | collective-permute-start | bytes 98312 | tf_op jit(solution)/shard_map/ppermute | solution.py:31
  297.4 5.2 collective-permute-start.8
  306.2 12.9 %collective-permute-start.9 = (f32[4,128,136]{2,0,1:T(4,128)}, f32[4,128,136]{2,0,1:T(4,128)}, u32[]{:S(2)}, u32[]{:S(2)}) collective-permute-start(f32[4,128,136]{2,0,1:T(4,128)} %get-tuple-element.59), channel_id=1, source_target_pairs={{0,1},{1,2},{2,3},{4,5},{5,6},{6,7},{8,9},{9,10},{10,11},{12,13},{... | collective-permute-start | bytes 835592 | tf_op jit(solution)/shard_map/ppermute | solution.py:31
  308.2 16.3 %collective-permute-start.10 = (f32[4,128,136]{2,0,1:T(4,128)}, f32[4,128,136]{2,0,1:T(4,128)}, u32[]{:S(2)}, u32[]{:S(2)}) collective-permute-start(f32[4,128,136]{2,0,1:T(4,128)} %get-tuple-element.60), channel_id=1, source_target_pairs={{1,0},{2,1},{3,2},{5,4},{6,5},{7,6},{9,8},{10,9},{11,10},{13,12},{... | collective-permute-start | bytes 835592 | tf_op jit(solution)/shard_map/ppermute | solution.py:34
  309.5 46.2 %all-to-all-start.5 = ((f32[16,128,128]{2,0,1:T(8,128)}), f32[16,128,128]{2,0,1:T(8,128)S(1)}, u32[]{:S(2)}, u32[]{:S(2)}) async-start(f32[16,128,128]{2,0,1:T(8,128)} %fusion.111), calls=%async_computation.5 | async-start | bytes 2097152 | tf_op jit(solution)/shard_map/all_to_all | solution.py:141
  346.8 13.7 %collective-permute-start.13 = (f32[16,32,128]{2,1,0:T(8,128)}, f32[16,32,128]{2,1,0:T(8,128)}, u32[]{:S(2)}, u32[]{:S(2)}) collective-permute-start(f32[16,32,128]{2,1,0:T(8,128)} %bitcast.312), channel_id=1, source_target_pairs={{0,3},{1,2},{2,1},{3,0},{4,7},{5,6},{6,5},{7,4},{8,11},{9,10},{10,... | collective-permute-start | bytes 786440 | tf_op jit(solution)/shard_map/ppermute | solution.py:154
  347.9 16.1 %collective-permute-start.11 = (f32[16,32,128]{2,1,0:T(8,128)}, f32[16,32,128]{2,1,0:T(8,128)}, u32[]{:S(2)}, u32[]{:S(2)}) collective-permute-start(f32[16,32,128]{2,1,0:T(8,128)} %bitcast.314), channel_id=1, source_target_pairs={{0,1},{1,0},{2,3},{3,2},{4,5},{5,4},{6,7},{7,6},{8,9},{9,8},{10,11... | collective-permute-start | bytes 786440 | tf_op jit(solution)/shard_map/ppermute | solution.py:154
  349.6 23.5 %collective-permute-start.12 = (f32[16,32,128]{2,1,0:T(8,128)}, f32[16,32,128]{2,1,0:T(8,128)}, u32[]{:S(2)}, u32[]{:S(2)}) collective-permute-start(f32[16,32,128]{2,1,0:T(8,128)} %bitcast.313), channel_id=1, source_target_pairs={{0,2},{1,3},{2,0},{3,1},{4,6},{5,7},{6,4},{7,5},{8,10},{9,11},{10,... | collective-permute-start | bytes 786440 | tf_op jit(solution)/shard_map/ppermute | solution.py:154
  355.7 35.0 %all-to-all-start.6 = ((f32[16,128,128]{2,0,1:T(8,128)}), f32[16,128,128]{2,0,1:T(8,128)S(1)}, u32[]{:S(2)}, u32[]{:S(2)}) async-start(f32[16,128,128]{2,0,1:T(8,128)} %get-tuple-element.57), calls=%async_computation.6 | async-start | bytes 2097152 | tf_op jit(solution)/shard_map/all_to_all | solution.py:140
  359.8 13.2 %copy-start.78 = (f32[16,2,2,128]{3,0,2,1:T(8,128)}, f32[16,2,2,128]{3,0,2,1:T(8,128)S(1)}, u32[]{:S(2)}) copy-start(f32[16,2,2,128]{3,0,2,1:T(8,128)S(1)} %copy.1323) | copy-start | bytes 98308
  390.7 129.9 %all-to-all-start.8 = ((f32[16,128,128]{2,0,1:T(8,128)}), f32[16,128,128]{2,0,1:T(8,128)}, u32[]{:S(2)}, u32[]{:S(2)}) async-start(f32[16,128,128]{2,0,1:T(8,128)} %fusion.111), calls=%async_computation.8 | async-start | bytes 2097152 | tf_op jit(solution)/shard_map/all_to_all | solution.py:166
  446.0 7.4 %copy-start.4 = (f32[16,16,512]{1,0,2:T(8,128)S(1)}, f32[16,16,512]{1,0,2:T(8,128)}, u32[]{:S(2)}) copy-start(f32[16,16,512]{1,0,2:T(8,128)} %get-tuple-element.18) | copy-start | bytes 1572868
  520.6 6.4 %copy-start.25 = (f32[64,32,128]{2,1,0:T(8,128)S(1)}, f32[64,32,128]{2,1,0:T(8,128)}, u32[]{:S(2)}) copy-start(f32[64,32,128]{2,1,0:T(8,128)} %copy-done.24) | copy-start | bytes 3145732
  520.6 6.4 %copy-start.27 = (f32[64,32,128]{2,1,0:T(8,128)S(1)}, f32[64,32,128]{2,1,0:T(8,128)}, u32[]{:S(2)}) copy-start(f32[64,32,128]{2,1,0:T(8,128)} %copy-done.26) | copy-start | bytes 3145732
  520.6 6.4 %copy-start.29 = (f32[64,32,128]{2,1,0:T(8,128)S(1)}, f32[64,32,128]{2,1,0:T(8,128)}, u32[]{:S(2)}) copy-start(f32[64,32,128]{2,1,0:T(8,128)} %get-tuple-element.91) | copy-start | bytes 3145732
  520.7 17.8 %all-to-all-start.7 = ((f32[8,1,32768]{2,1,0:T(1,128)}), f32[8,1,32768]{2,1,0:T(1,128)}, u32[]{:S(2)}, u32[]{:S(2)}) async-start(f32[8,1,32768]{2,1,0:T(1,128)} %reshape.303), calls=%async_computation.7 | async-start | bytes 2097152 | tf_op jit(solution)/shard_map/all_to_all | solution.py:144
  529.7 16.9 %copy-start.46 = (f32[16,64,128]{2,0,1:T(8,128)S(1)}, f32[16,64,128]{2,0,1:T(8,128)}, u32[]{:S(2)}) copy-start(f32[16,64,128]{2,0,1:T(8,128)} %copy-done.45) | copy-start | bytes 1572868
  529.7 16.9 %copy-start.48 = (f32[16,64,128]{2,0,1:T(8,128)S(1)}, f32[16,64,128]{2,0,1:T(8,128)}, u32[]{:S(2)}) copy-start(f32[16,64,128]{2,0,1:T(8,128)} %copy-done.47) | copy-start | bytes 1572868
  529.7 16.9 %copy-start.56 = (f32[16,64,128]{2,0,1:T(8,128)S(1)}, f32[16,64,128]{2,0,1:T(8,128)}, u32[]{:S(2)}) copy-start(f32[16,64,128]{2,0,1:T(8,128)} %copy-done.55) | copy-start | bytes 1572868
  529.7 16.9 %copy-start.60 = (f32[16,64,128]{2,0,1:T(8,128)S(1)}, f32[16,64,128]{2,0,1:T(8,128)}, u32[]{:S(2)}) copy-start(f32[16,64,128]{2,0,1:T(8,128)} %copy-done.59) | copy-start | bytes 1572868
  538.4 30.9 %all-to-all-start.9 = ((f32[64,32,128]{2,1,0:T(8,128)}), f32[64,32,128]{2,1,0:T(8,128)S(1)}, u32[]{:S(2)}, u32[]{:S(2)}) async-start(f32[64,32,128]{2,1,0:T(8,128)} %bitcast.199), calls=%async_computation.9 | async-start | bytes 2097152 | tf_op jit(solution)/shard_map/all_to_all | solution.py:169
  (70 other events, 158.8 us)
